TPU v7x, 512 devices: a whole 4x4x16 slice. The times are simulated.
512 devices in a mesh: rep: 4 (over x), fsdp: 16 (over z), tp: 8 (over y, core).
Axes of the slice: x: 4, y: 4, z: 16, core: 2. Of those that a mesh axis runs over, the one named last changes fastest.
Arguments:
- tracker: bfloat16 [4, 4096, 14336], P('rep', 'fsdp', 'tp'), may hold values from -20 to 20
- grad_delta: bfloat16 [4, 4096, 14336], P('rep', 'fsdp', 'tp'), may hold values from -20 to 20
- momentum: bfloat16 [4, 4096, 14336], P('rep', 'fsdp', 'tp'), may hold values from -20 to 20
- q_basis: bfloat16 [4, 14336, 512], P('rep', 'tp', 'fsdp'), may hold values from -0.046875 to 0.046875
- mix_counts: int32 [4, 3], replicated, may hold values from 1 to 8
Outputs:
- new_tracker: bfloat16 [4, 4096, 14336], P('rep', 'fsdp', 'tp')
- new_momentum: bfloat16 [4, 4096, 14336], P('rep', 'fsdp', 'tp')
- left_basis: bfloat16 [4, 4096, 512], P('rep', 'fsdp')
- q_new: bfloat16 [4, 14336, 512], P('rep', 'tp', 'fsdp')
All inputs are finite; a program needn't handle non-finite values.
Results may differ from a plain program's by a relative error of at most 0.0061.
Values may be sent and summed in bfloat16 or wider, within the bound.
A program may use at most 64 MiB of HBM per device.

v0:
```python
import jax
import jax.numpy as jnp
from jax import lax
from jax.sharding import PartitionSpec as P

D = 4096
FF = 14336


def extended(block, sides, width):
    for axis, dim in sides:
        count = lax.axis_size(axis)
        forward = [(i, i + 1) for i in range(count - 1)]
        forward.append((count - 1, 0))
        backward = [(target, source) for source, target in forward]
        low = lax.ppermute(
            lax.slice_in_dim(block, block.shape[dim] - width, None, axis=dim), axis, forward
        )
        high = lax.ppermute(lax.slice_in_dim(block, 0, width, axis=dim), axis, backward)
        block = jnp.concatenate([low, block, high], axis=dim)
    return block


def orthonormal(pmat, gram):
    factor = jnp.linalg.cholesky(gram)
    solved = jax.scipy.linalg.solve_triangular(factor, pmat.T, lower=True).T
    return (solved * jnp.sqrt(jnp.float32(D))).astype(jnp.bfloat16)


def local(tracker, grad_delta, momentum, q_basis, mix_counts):
    agent = lax.axis_index("rep")
    counts = mix_counts.astype(jnp.float32)
    select = (jnp.arange(counts.shape[0]) == agent).astype(jnp.float32)
    mine = jnp.sum(select[:, None] * counts, axis=0)
    weights = mine / jnp.sum(mine)
    near = extended(tracker, (("rep", 0),), 1)
    mixed = (
        weights[0] * near[1].astype(jnp.float32)
        + weights[1] * near[0].astype(jnp.float32)
        + weights[2] * near[2].astype(jnp.float32)
    )
    tracked = mixed + grad_delta[0].astype(jnp.float32)
    new_tracker = tracked.astype(jnp.bfloat16)
    accum = momentum[0].astype(jnp.float32) + tracked
    accum_b = accum.astype(jnp.bfloat16)
    scale = 1.0 / jnp.sqrt(jnp.float32(D))
    basis_full = lax.all_gather(q_basis, "fsdp", axis=2, tiled=True)[0]
    partial_left = jnp.dot(accum_b, basis_full, preferred_element_type=jnp.float32)
    pmat = lax.psum(partial_left, "tp")
    gram_part = jnp.dot(pmat.T, pmat, precision=lax.Precision.HIGHEST)
    gram = lax.psum(gram_part, "fsdp")
    left_b = orthonormal(pmat, gram)
    block = left_b
    product = lax.dot_general(
        block, accum_b, (((0,), (0,)), ((), ())), preferred_element_type=jnp.float32
    )
    right_t = lax.psum_scatter(product * scale, "fsdp", scatter_dimension=0, tiled=True)
    squares = lax.psum(jnp.sum(right_t * right_t, axis=1), "tp")
    rms = jnp.sqrt(squares / FF) + 1e-06
    q_new = (right_t / rms[:, None]).T.astype(jnp.bfloat16)
    right_b = right_t.astype(jnp.bfloat16)
    block = left_b
    feed = jnp.dot(
        block,
        lax.all_gather(right_b, "fsdp", axis=0, tiled=True),
        preferred_element_type=jnp.float32,
    )
    new_momentum = (accum - 0.5 * scale * feed).astype(jnp.bfloat16)
    return (new_tracker[None], new_momentum[None], left_b[None], q_new[None])


def solution(mesh):
    in_specs = (
        P("rep", "fsdp", "tp"),
        P("rep", "fsdp", "tp"),
        P("rep", "fsdp", "tp"),
        P("rep", "tp", "fsdp"),
        P(),
    )
    out_specs = (
        P("rep", "fsdp", "tp"),
        P("rep", "fsdp", "tp"),
        P("rep", "fsdp", None),
        P("rep", "tp", "fsdp"),
    )
    return jax.shard_map(local, mesh=mesh, in_specs=in_specs, out_specs=out_specs, check_vma=False)
```

profile of v0, /device:TPU:6, one launch (start us, length us, event | category | flops | bytes accessed | tf_op | source)
XLA Modules:
  0.0 640.5 jit_solution(14598845073682928262)
XLA Ops:
  7.9 2.7 collective-permute-start.1
  10.7 6.9 %collective-permute-start = (bf16[1,256,1792]{2,1,0:T(8,128)(2,1)}, bf16[1,256,1792]{2,1,0:T(8,128)(2,1)S(1)}, u32[]{:S(2)}, u32[]{:S(2)}) collective-permute-start(bf16[1,256,1792]{2,1,0:T(8,128)(2,1)} %param.5), channel_id=1, source_target_pairs={{0,128},{128,256},{256,384},{384,0},{1,129},{129,257},{257,385},{3... | collective-permute-start | bytes 2752520 | tf_op jit(solution)/shard_map/ppermute | solution.py:16
  17.7 1.4 fusion.37
  20.3 13.1 %collective-permute-done.1 = bf16[1,256,1792]{2,1,0:T(8,128)(2,1)S(1)} collective-permute-done((bf16[1,256,1792]{2,1,0:T(8,128)(2,1)}, bf16[1,256,1792]{2,1,0:T(8,128)(2,1)S(1)}, u32[]{:S(2)}, u32[]{:S(2)}) %collective-permute-start.1) | collective-permute-done | bytes 917536 | tf_op jit(solution)/shard_map/ppermute | solution.py:19
  33.4 1.3 collective-permute-done
  35.6 5.5 fusion.44
  41.1 46.1 %all-gather.3.cloned.1.call-done = bf16[1,1792,512]{1,2,0:T(8,128)(2,1)} async-done(((bf16[1,1792,32]{1,2,0:T(8,128)(2,1)}), bf16[1,1792,512]{1,2,0:T(8,128)(2,1)}) %all-gather.3.cloned.1.call-update) | async-done | bytes 1835024 | tf_op jit(solution)/shard_map/all_gather | solution.py:47
  87.2 3.0 fusion.3
  90.2 73.3 %all-reduce.4.cloned.1.call-done = f32[256,512]{1,0:T(8,128)} async-done(((f32[256,512]{1,0:T(8,128)}), f32[256,512]{1,0:T(8,128)}) %all-reduce.4.cloned.1.call-update) | async-done | bytes 524304 | tf_op jit(solution)/shard_map/psum | solution.py:49
  163.5 3.3 fusion.47
  167.1 138.0 %all-reduce.6.cloned.1.call-done = f32[512,512]{0,1:T(8,128)} async-done(((f32[512,512]{0,1:T(8,128)}), f32[512,512]{0,1:T(8,128)}) %all-reduce.6.cloned.1.call-update) | async-done | bytes 1048592 | tf_op jit(solution)/shard_map/psum | solution.py:51
  305.1 2.6 copy.10
  307.7 1.8 fusion.5
  309.4 1.0 copy-done.4
  310.4 11.7 %cholesky.104 = f32[128,128]{1,0:T(8,128)S(1)} custom-call(f32[128,128]{1,0:T(8,128)S(1)} %cholesky.266), custom_call_target="Cholesky" | custom-call | tf_op jit(solution)/shard_map/jit(cholesky)/cholesky | solution.py:25
  322.2 1.2 cholesky.224
  323.4 9.8 %custom-call.31 = f32[1,128,128]{1,2,0:T(8,128)S(1)} custom-call(f32[1,128,128]{2,1,0:T(8,128)S(1)} %get-tuple-element.41), custom_call_target="InvertDiagBlocksLowerTriangular" | custom-call | tf_op jit(solution)/shard_map/jit(cholesky)/cholesky | solution.py:25
  333.2 2.0 constant_dynamic-update-slice_fusion.3
  335.1 1.3 convolution_subtract_fusion
  336.4 11.7 %cholesky.217 = f32[128,128]{1,0:T(8,128)S(1)} custom-call(f32[128,128]{1,0:T(8,128)S(1)} %cholesky.270), custom_call_target="Cholesky" | custom-call | tf_op jit(solution)/shard_map/jit(cholesky)/cholesky | solution.py:25
  348.8 10.0 %custom-call.32 = f32[1,128,128]{1,2,0:T(8,128)S(1)} custom-call(f32[1,128,128]{2,1,0:T(8,128)S(1)} %get-tuple-element.38), custom_call_target="InvertDiagBlocksLowerTriangular" | custom-call | tf_op jit(solution)/shard_map/jit(cholesky)/cholesky | solution.py:25
  358.8 0.9 convolution_dynamic-update-slice_fusion
  359.7 1.4 convolution_subtract_fusion.3
  361.2 11.7 %cholesky.238 = f32[128,128]{1,0:T(8,128)S(1)} custom-call(f32[128,128]{1,0:T(8,128)S(1)} %cholesky.275), custom_call_target="Cholesky" | custom-call | tf_op jit(solution)/shard_map/jit(cholesky)/cholesky | solution.py:25
  373.5 9.8 %custom-call.33 = f32[1,128,128]{1,2,0:T(8,128)S(1)} custom-call(f32[1,128,128]{2,1,0:T(8,128)S(1)} %get-tuple-element.35), custom_call_target="InvertDiagBlocksLowerTriangular" | custom-call | tf_op jit(solution)/shard_map/jit(cholesky)/cholesky | solution.py:25
  384.2 1.4 convolution_subtract_fusion.5
  385.6 11.7 %cholesky.255 = f32[128,128]{1,0:T(8,128)S(1)} custom-call(f32[128,128]{1,0:T(8,128)S(1)} %convolution_subtract_fusion.5), custom_call_target="Cholesky" | custom-call | tf_op jit(solution)/shard_map/jit(cholesky)/cholesky | solution.py:25
  402.5 2.6 select_select_fusion
  405.1 14.5 %while.1 = (s32[]{:T(128)}, f32[512,512]{1,0:T(8,128)}, s32[4,2]{0,1:T(2,128)S(1)}, f32[4,128,128]{2,1,0:T(8,128)}, s32[]{:T(128)}) while((s32[]{:T(128)}, f32[512,512]{1,0:T(8,128)}, s32[4,2]{0,1:T(2,128)S(1)}, f32[4,128,128]{2,1,0:T(8,128)}, s32[]{:T(128)}) %tuple.37), condition=%wide.while_cond, body=%wide.while_body.sunk | while | flops 2 | bytes 132205 | solution.py:26
  405.8 3.0 bitcast_dynamic-update-slice_fusion.2
  409.4 3.0 bitcast_dynamic-update-slice_fusion.2
  413.0 3.0 bitcast_dynamic-update-slice_fusion.2
  416.7 2.9 bitcast_dynamic-update-slice_fusion.2
  419.6 40.8 %custom-call.34 = f32[4,128,128]{1,2,0:T(8,128)} custom-call(f32[4,128,128]{2,1,0:T(8,128)} %get-tuple-element.11), custom_call_target="InvertDiagBlocksLowerTriangular" | custom-call | tf_op jit(solution)/shard_map/jit(_solve_triangular)/triangular_solve | solution.py:26
  460.3 1.1 fusion.23
  461.5 1.2 convolution_subtract_fusion.4
  462.7 1.2 fusion.31
  463.9 1.5 convolution_subtract_fusion.2
  465.4 1.2 fusion.29
  466.6 1.8 convolution_subtract_fusion.1
  468.4 1.2 fusion.28
  469.5 2.5 convolution_multiply_fusion
  472.1 74.9 %reduce-scatter.2.cloned.1.call-done = f32[32,1792]{1,0:T(8,128)} async-done(((f32[512,1792]{1,0:T(8,128)}), f32[32,1792]{1,0:T(8,128)}) %reduce-scatter.2.cloned.1.call-update) | async-done | bytes 229392 | tf_op jit(solution)/shard_map/reduce_scatter | solution.py:57
  547.0 1.1 multiply_reduce_fusion
  548.1 12.4 %psum.23 = f32[32]{0:T(128)S(1)} all-reduce(f32[32]{0:T(128)S(1)} %multiply_reduce_fusion), channel_id=1, replica_groups=mesh['rep'=4,'fsdp'=16,'tp'=8] {'tp'}, use_global_device_ids=true, to_apply=%region_14.15 | all-reduce | flops 32 | bytes 256 | tf_op jit(solution)/shard_map/psum | solution.py:58
  560.5 1.8 fusion.27
  563.2 67.6 %all-gather.5.cloned.1.call-done = bf16[512,1792]{1,0:T(8,128)(2,1)} async-done(((bf16[32,1792]{1,0:T(8,128)(2,1)}), bf16[512,1792]{1,0:T(8,128)(2,1)}) %all-gather.5.cloned.1.call-update) | async-done | bytes 1835024 | tf_op jit(solution)/shard_map/all_gather | solution.py:65
  630.9 3.1 fusion.2
  (51 shorter events, 11.7 us)
Async XLA Ops:
  7.2 80.0 %all-gather.3.cloned.1.call-start = ((), (), s32[]{:S(2)}) async-start(), calls=%async_computation.1 | async-start | bytes 1949696 | tf_op jit(solution)/shard_map/all_gather | solution.py:47
  7.9 155.6 %all-reduce.4.cloned.1.call-start = ((), (), s32[]{:S(2)}) async-start(), calls=%async_computation.2 | async-start | bytes 1048576 | tf_op jit(solution)/shard_map/psum | solution.py:49
  7.9 25.4 %collective-permute-start.1 = (bf16[1,256,1792]{2,1,0:T(8,128)(2,1)}, bf16[1,256,1792]{2,1,0:T(8,128)(2,1)S(1)}, u32[]{:S(2)}, u32[]{:S(2)}) collective-permute-start(bf16[1,256,1792]{2,1,0:T(8,128)(2,1)} %param.5), channel_id=1, source_target_pairs={{128,0},{256,128},{384,256},{0,384},{129,1},{257,129},{385,257},{1... | collective-permute-start | bytes 2752520 | tf_op jit(solution)/shard_map/ppermute | solution.py:19
  10.7 23.9 %collective-permute-start = (bf16[1,256,1792]{2,1,0:T(8,128)(2,1)}, bf16[1,256,1792]{2,1,0:T(8,128)(2,1)S(1)}, u32[]{:S(2)}, u32[]{:S(2)}) collective-permute-start(bf16[1,256,1792]{2,1,0:T(8,128)(2,1)} %param.5), channel_id=1, source_target_pairs={{0,128},{128,256},{256,384},{384,0},{1,129},{129,257},{257,385},{3... | collective-permute-start | bytes 2752520 | tf_op jit(solution)/shard_map/ppermute | solution.py:16
  33.4 1.3 copy-start.5
  34.6 0.9 copy-start.6
  35.6 51.6 %copy-start = (bf16[1,256,1792]{2,1,0:T(8,128)(2,1)S(1)}, bf16[1,256,1792]{2,1,0:T(8,128)(2,1)}, u32[]{:S(2)}) copy-start(bf16[1,256,1792]{2,1,0:T(8,128)(2,1)} %param.7) | copy-start | bytes 2752516
  90.2 214.9 %all-reduce.6.cloned.1.call-start = ((), (), s32[]{:S(2)}) async-start(), calls=%async_computation.3 | async-start | bytes 2097152 | tf_op jit(solution)/shard_map/psum | solution.py:51
  166.8 380.2 %reduce-scatter.2.cloned.1.call-start = ((), (), s32[]{:S(2)}) async-start(), calls=%async_computation.4 | async-start | bytes 3899392 | tf_op jit(solution)/shard_map/reduce_scatter | solution.py:57
  309.4 1.0 copy-start.4
  373.5 86.8 %copy-start.1 = (f32[256,512]{1,0:T(8,128)S(1)}, f32[256,512]{1,0:T(8,128)}, u32[]{:S(2)}) copy-start(f32[256,512]{1,0:T(8,128)} %all-reduce.4.cloned.1.call-done) | copy-start | bytes 1572868
  466.5 3.0 copy-start.2
  472.0 90.3 %copy-start.3 = (f32[128,256]{1,0:T(8,128)S(1)}, f32[128,256]{1,0:T(8,128)}, u32[]{:S(2)}) copy-start(f32[128,256]{1,0:T(8,128)} %copy-done.2) | copy-start | bytes 393220
  472.0 158.8 %all-gather.5.cloned.1.call-start = ((), (), s32[]{:S(2)}) async-start(), calls=%async_computation.5 | async-start | bytes 1949696 | tf_op jit(solution)/shard_map/all_gather | solution.py:65
Sparse Core Ops, SparseCore 0:
  10.1 77.0 all-gather.2
  90.3 73.1 all-reduce.3
  167.0 138.0 all-reduce.5
  472.1 74.8 reduce-scatter.1
  562.4 68.3 all-gather.4
where the time goes:
time: 642 us; the launch traced here: 640 us
  waiting for transfers between devices  415 us (65%)
  other arithmetic  136 us (21%)
  matrix products  28.8 us (4%)
  local copies, waits for them, and re-layouts  21.6 us (3%)
  between operations  16.5 us (3%)
  blocking collectives  12.4 us (2%)
  starting transfers between devices  10.1 us (2%)
    psum x1, waiting for transfers between devices, local(): gram = lax.psum(gram_part, 'fsdp')  138 us
    another operation x14, other arithmetic, orthonormal(): factor = jnp.linalg.cholesky(gram)  80.4 us
    reduce_scatter x1, waiting for transfers between devices, local(): lax.psum_scatter(product * scale, 'fsdp', scatter_dimension=0, tiled=True)  74.9 us
    psum x1, waiting for transfers between devices, local(): pmat = lax.psum(partial_left, 'tp')  73.3 us
    all_gather x1, waiting for transfers between devices, local(): lax.all_gather(right_b, 'fsdp', axis=0, tiled=True)  67.6 us
    all_gather x1, waiting for transfers between devices, local(): basis_full = lax.all_gather(q_basis, 'fsdp', axis=2, tiled=True)[0]  46.1 us
    another operation x3, other arithmetic, orthonormal(): solved = jax.scipy.linalg.solve_triangular(factor, pmat.T, lower=True).T  43.4 us
    another operation x12, local copies, waits for them, and re-layouts  14.5 us
  transfers between devices with their start and end apart: 7, of which 7 were waited for; matrix products, arithmetic and copies ran while one was open for 1% of the time, Pallas kernels for 0%

commit v1 on v0

--- a/solution.py
+++ b/solution.py
@@ -1,6 +1,8 @@
 import jax
 import jax.numpy as jnp
 from jax import lax
+from jax.experimental import pallas as pl
+from jax.experimental.pallas import tpu as pltpu
 from jax.sharding import PartitionSpec as P
 
 D = 4096
@@ -21,10 +23,85 @@
     return block
 
 
-def orthonormal(pmat, gram):
-    factor = jnp.linalg.cholesky(gram)
-    solved = jax.scipy.linalg.solve_triangular(factor, pmat.T, lower=True).T
-    return (solved * jnp.sqrt(jnp.float32(D))).astype(jnp.bfloat16)
+NB = 128
+HI = lax.Precision.HIGHEST
+
+def factor_inverse(load, store):
+    G = NB // 8
+    sub = lax.broadcasted_iota(jnp.int32, (8, NB), 0)
+    lane = lax.broadcasted_iota(jnp.int32, (8, NB), 1)
+    A = [load(h) for h in range(G)]
+    W = [jnp.where(lane == sub + 8 * h, 1.0, 0.0).astype(jnp.float32) for h in range(G)]
+    row = lambda x, a: jnp.broadcast_to(x[a:a + 1, :], (8, NB))
+    colb = lambda x, j: jnp.broadcast_to(x[:, j:j + 1], (8, NB))
+    for g in range(G):
+        j0 = 8 * g
+        RA, RW = A[g], W[g]
+        E = [colb(RA, j0 + a) for a in range(8)]
+        FA, FW = RA, RW
+        for a in range(8):
+            ra, rw = row(RA, a), row(RW, a)
+            inv = 1.0 / row(E[a], a)
+            hit = sub == a
+            FA = jnp.where(hit, ra, FA)
+            FW = jnp.where(hit, rw, FW)
+            sa, sw = ra * inv, rw * inv
+            RA = jnp.where(hit, sa, RA - E[a] * sa)
+            RW = jnp.where(hit, sw, RW - E[a] * sw)
+            for b in range(a + 1, 8):
+                eb = row(E[b], a) * inv
+                E[b] = jnp.where(hit, eb, E[b] - E[a] * eb)
+        A[g], W[g] = FA, FW
+        SA = [row(RA, a) for a in range(8)]
+        SW = [row(RW, a) for a in range(8)]
+        for h in range(g + 1, G):
+            ah, wh, src = A[h], W[h], A[h]
+            for a in range(8):
+                c = colb(src, j0 + a)
+                ah = ah - c * SA[a]
+                wh = wh - c * SW[a]
+            A[h], W[h] = ah, wh
+    for g in range(G):
+        d = jnp.sum(jnp.where(lane == sub + 8 * g, A[g], 0.0), axis=1, keepdims=True)
+        store(g, W[g] * lax.rsqrt(d))
+
+def nt(a, b):
+    return lax.dot_general(a, b, (((1,), (1,)), ((), ())), precision=HI, preferred_element_type=jnp.float32)
+
+def solve_kernel(g_ref, p_ref, o_ref, t_ref, w_ref):
+    n = g_ref.shape[0]
+    m = p_ref.shape[0]
+    K = n // NB
+    t_ref[0:n, :] = g_ref[...]
+    t_ref[n:n + m, :] = p_ref[...]
+    def step(k, _):
+        base = pl.multiple_of(k * NB, NB)
+        def load(h):
+            return t_ref[pl.ds(pl.multiple_of(base + 8 * h, 8), 8), pl.ds(base, NB)]
+        def store(h, v):
+            w_ref[8 * h:8 * h + 8, :] = v
+        factor_inverse(load, store)
+        for kk in range(K):
+            @pl.when(k == kk)
+            def _():
+                lo, hi = kk * NB, (kk + 1) * NB
+                x = nt(t_ref[hi:, lo:hi], w_ref[...])
+                o_ref[:, lo:hi] = (x[n - hi:] * D ** 0.5).astype(jnp.bfloat16)
+                if kk + 1 < K:
+                    t_ref[hi:, hi:] = t_ref[hi:, hi:] - nt(x, x[:n - hi])
+        return 0
+    lax.fori_loop(0, K, step, 0)
+
+def left_solve(gram, pmat):
+    n, m = gram.shape[0], pmat.shape[0]
+    return pl.pallas_call(
+        solve_kernel,
+        out_shape=jax.ShapeDtypeStruct((m, n), jnp.bfloat16),
+        in_specs=[pl.BlockSpec(memory_space=pltpu.VMEM)] * 2,
+        out_specs=pl.BlockSpec(memory_space=pltpu.VMEM),
+        scratch_shapes=[pltpu.VMEM((n + m, n), jnp.float32), pltpu.VMEM((NB, NB), jnp.float32)],
+        compiler_params=pltpu.CompilerParams(vmem_limit_bytes=40 << 20),
+    )(gram, pmat)
 
 
 def local(tracker, grad_delta, momentum, q_basis, mix_counts):
@@ -49,7 +126,7 @@
     pmat = lax.psum(partial_left, "tp")
     gram_part = jnp.dot(pmat.T, pmat, precision=lax.Precision.HIGHEST)
     gram = lax.psum(gram_part, "fsdp")
-    left_b = orthonormal(pmat, gram)
+    left_b = left_solve(gram, pmat)
     block = left_b
     product = lax.dot_general(
         block, accum_b, (((0,), (0,)), ((), ())), preferred_element_type=jnp.float32

time: 642 us -> 502 us (0.78)
  other arithmetic: 136 us -> 10.4 us
  Pallas kernels: 0 us -> 23.3 us
  local copies, waits for them, and re-layouts: 21.6 us -> 2.81 us
  matrix products: 28.8 us -> 12.8 us
    another operation x17 -> x0, other arithmetic: 124 us -> none  [the longest x14 80.4 us: orthonormal(): factor = jnp.linalg.cholesky(gram)]
    pallas_call x0 -> x1, Pallas kernels: none -> 23.3 us  [left_solve(): pl.pallas_call(solve_kernel, out_shape=jax.ShapeDtypeStruct((m, n), jnp.b...]
    another operation x13 -> x0, matrix products: 17 us -> none  [the longest x7 9.13 us: orthonormal(): solved = jax.scipy.linalg.solve_triangular(factor, pmat.T, lower=True).T]
    another operation x17 -> x0, local copies, waits for them, and re-layouts: 15.7 us -> none
  transfers between devices with their start and end apart: 7 -> 7, of which waited for: 7 -> 7; matrix products, arithmetic and copies ran while one was open for 1% -> 2% of each run, Pallas kernels for 0% -> 0%
where the time goes in v1:
time: 502 us
  waiting for transfers between devices  416 us (83%)
  Pallas kernels  23.3 us (5%)
  between operations  13.8 us (3%)
  matrix products  12.8 us (3%)
  blocking collectives  12.4 us (2%)
  other arithmetic  10.4 us (2%)
  starting transfers between devices  9.89 us (2%)
    psum x1, waiting for transfers between devices, local(): gram = lax.psum(gram_part, 'fsdp')  138 us
    reduce_scatter x1, waiting for transfers between devices, local(): lax.psum_scatter(product * scale, 'fsdp', scatter_dimension=0, tiled=True)  74.8 us
    psum x1, waiting for transfers between devices, local(): pmat = lax.psum(partial_left, 'tp')  73.1 us
    all_gather x1, waiting for transfers between devices, local(): lax.all_gather(right_b, 'fsdp', axis=0, tiled=True)  68.9 us
    all_gather x1, waiting for transfers between devices, local(): basis_full = lax.all_gather(q_basis, 'fsdp', axis=2, tiled=True)[0]  46.1 us
    pallas_call x1, Pallas kernels, left_solve(): pl.pallas_call(solve_kernel, out_shape=jax.ShapeDtypeStruct((m, n), jnp.b...  23.3 us
    ppermute x1, waiting for transfers between devices, extended(): lax.ppermute(lax.slice_in_dim(block, 0, width, axis=dim), axis, backward)  13 us
    psum x1, blocking collectives, local(): squares = lax.psum(jnp.sum(right_t * right_t, axis=1), 'tp')  12.4 us
  transfers between devices with their start and end apart: 7, of which 7 were waited for; matrix products, arithmetic and copies ran while one was open for 2% of the time, Pallas kernels for 0%

profile of v1, /device:TPU:6, one launch (start us, length us, event | category | flops | bytes accessed | tf_op | source)
XLA Modules:
  0.0 501.7 jit_solution(18443331699472375680)
XLA Ops:
  7.2 0.0 all-gather.3.cloned.1.call-start
  7.2 0.7 all-gather.3.cloned.1.call-update
  7.9 0.0 all-reduce.3.cloned.1.call-start
  7.9 2.7 collective-permute-start.1
  10.7 6.9 %collective-permute-start = (bf16[1,256,1792]{2,1,0:T(8,128)(2,1)}, bf16[1,256,1792]{2,1,0:T(8,128)(2,1)S(1)}, u32[]{:S(2)}, u32[]{:S(2)}) collective-permute-start(bf16[1,256,1792]{2,1,0:T(8,128)(2,1)} %param.5), channel_id=1, source_target_pairs={{0,128},{128,256},{256,384},{384,0},{1,129},{129,257},{257,385},{3... | collective-permute-start | bytes 2752520 | tf_op jit(solution)/shard_map/ppermute | solution.py:18
  17.7 1.4 fusion.8
  19.0 0.6 broadcast_divide_fusion
  19.7 0.7 fusion.11
  20.3 13.0 %collective-permute-done.1 = bf16[1,256,1792]{2,1,0:T(8,128)(2,1)S(1)} collective-permute-done((bf16[1,256,1792]{2,1,0:T(8,128)(2,1)}, bf16[1,256,1792]{2,1,0:T(8,128)(2,1)S(1)}, u32[]{:S(2)}, u32[]{:S(2)}) %collective-permute-start.1) | collective-permute-done | bytes 917536 | tf_op jit(solution)/shard_map/ppermute | solution.py:21
  33.4 0.0 copy-start.4
  33.4 1.3 collective-permute-done
  34.6 0.0 copy-start.5
  34.6 0.0 copy-done.4
  34.6 0.9 copy-done.5
  35.6 0.0 copy-start.2
  35.6 5.6 %fusion.10 = (bf16[1,256,1792]{2,1,0:T(8,128)(2,1)}, f32[1,256,1792]{2,1,0:T(8,128)S(1)}) fusion(bf16[1,256,1792]{2,1,0:T(8,128)(2,1)} %param.6, bf16[1,256,1792]{2,1,0:T(8,128)(2,1)} %copy-done.4, f32[]{:T(128)} %bitcast.2, bf16[1,256,1792]{2,1,0:T(8,128)(2,1)} %copy-done.5, f32[]{:T(128)} %bitcast.1, bf16[1,256,1792]{2,1,0:T(8,128)(2,1)} %param.5, f32[]{:T(128)} %bitcast), kind=kLoop, calls=%fused_computation.21 | loop fusion | flops 5046272 | bytes 6422540 | tf_op jit(solution)/shard_map/convert_element_type | solution.py:120
  41.1 46.1 %all-gather.3.cloned.1.call-done = bf16[1,1792,512]{1,2,0:T(8,128)(2,1)} async-done(((bf16[1,1792,32]{1,2,0:T(8,128)(2,1)}), bf16[1,1792,512]{1,2,0:T(8,128)(2,1)}) %all-gather.3.cloned.1.call-update) | async-done | bytes 1835024 | tf_op jit(solution)/shard_map/all_gather | solution.py:124
  87.3 0.0 copy-done.2
  87.3 3.0 fusion.3
  90.2 0.0 all-reduce.3.cloned.1.call-update
  90.3 0.0 all-reduce.5.cloned.1.call-start
  90.3 73.1 %all-reduce.3.cloned.1.call-done.p_ref = f32[256,512]{1,0:T(8,128)} async-done(((f32[256,512]{1,0:T(8,128)}), f32[256,512]{1,0:T(8,128)}) %all-reduce.3.cloned.1.call-update) | async-done | bytes 524304 | tf_op jit(solution)/shard_map/psum | solution.py:126
  163.4 0.0 copy-start
  163.4 3.3 fusion.12
  166.7 0.0 all-reduce.5.cloned.1.call-update
  166.8 0.0 reduce-scatter.2.cloned.1.call-start
  166.8 138.2 %all-reduce.5.cloned.1.call-done.g_ref = f32[512,512]{1,0:T(8,128)} async-done(((f32[512,512]{1,0:T(8,128)}), f32[512,512]{1,0:T(8,128)}) %all-reduce.5.cloned.1.call-update) | async-done | bytes 1048592 | tf_op jit(solution)/shard_map/psum | solution.py:128
  305.0 0.0 copy-done
  305.0 0.0 copy-start.1
  305.0 1.2 copy-done.1
  306.3 23.3 %shard_map.84 = bf16[256,512]{1,0:T(8,128)(2,1)} custom-call(f32[512,512]{1,0:T(8,128)S(1)} %copy-done.1, f32[256,512]{1,0:T(8,128)S(1)} %copy-done), custom_call_target="tpu_custom_call" | custom-call | tf_op jit(solution)/shard_map/pallas_call | solution.py:97
  329.6 3.4 convolution_multiply_fusion
  333.0 0.0 copy-start.3
  333.0 0.0 reduce-scatter.2.cloned.1.call-update
  333.0 0.0 all-gather.5.cloned.1.call-start
  333.1 74.8 %reduce-scatter.2.cloned.1.call-done = f32[32,1792]{1,0:T(8,128)} async-done(((f32[512,1792]{1,0:T(8,128)}), f32[32,1792]{1,0:T(8,128)}) %reduce-scatter.2.cloned.1.call-update) | async-done | bytes 229392 | tf_op jit(solution)/shard_map/reduce_scatter | solution.py:134
  407.9 1.1 multiply_reduce_fusion
  409.0 12.4 %psum.23 = f32[32]{0:T(128)S(1)} all-reduce(f32[32]{0:T(128)S(1)} %multiply_reduce_fusion), channel_id=1, replica_groups=mesh['rep'=4,'fsdp'=16,'tp'=8] {'tp'}, use_global_device_ids=true, to_apply=%region_6.0 | all-reduce | flops 32 | bytes 256 | tf_op jit(solution)/shard_map/psum | solution.py:135
  421.4 1.8 fusion.7
  423.2 0.0 all-gather.5.cloned.1.call-update
  423.2 68.9 %all-gather.5.cloned.1.call-done = bf16[512,1792]{1,0:T(8,128)(2,1)} async-done(((bf16[32,1792]{1,0:T(8,128)(2,1)}), bf16[512,1792]{1,0:T(8,128)(2,1)}) %all-gather.5.cloned.1.call-update) | async-done | bytes 1835024 | tf_op jit(solution)/shard_map/all_gather | solution.py:142
  492.1 0.0 copy-done.3
  492.1 3.1 fusion.2
  (2 shorter events, 0.0 us)
Async XLA Ops:
  7.2 80.1 %all-gather.3.cloned.1.call-start = ((), (), s32[]{:S(2)}) async-start(), calls=%async_computation.1 | async-start | bytes 1949696 | tf_op jit(solution)/shard_map/all_gather | solution.py:124
  7.9 155.5 %all-reduce.3.cloned.1.call-start = ((), (), s32[]{:S(2)}) async-start(), calls=%async_computation.2 | async-start | bytes 1048576 | tf_op jit(solution)/shard_map/psum | solution.py:126
  7.9 25.4 %collective-permute-start.1 = (bf16[1,256,1792]{2,1,0:T(8,128)(2,1)}, bf16[1,256,1792]{2,1,0:T(8,128)(2,1)S(1)}, u32[]{:S(2)}, u32[]{:S(2)}) collective-permute-start(bf16[1,256,1792]{2,1,0:T(8,128)(2,1)} %param.5), channel_id=1, source_target_pairs={{128,0},{256,128},{384,256},{0,384},{129,1},{257,129},{385,257},{1... | collective-permute-start | bytes 2752520 | tf_op jit(solution)/shard_map/ppermute | solution.py:21
  10.7 23.9 %collective-permute-start = (bf16[1,256,1792]{2,1,0:T(8,128)(2,1)}, bf16[1,256,1792]{2,1,0:T(8,128)(2,1)S(1)}, u32[]{:S(2)}, u32[]{:S(2)}) collective-permute-start(bf16[1,256,1792]{2,1,0:T(8,128)(2,1)} %param.5), channel_id=1, source_target_pairs={{0,128},{128,256},{256,384},{384,0},{1,129},{129,257},{257,385},{3... | collective-permute-start | bytes 2752520 | tf_op jit(solution)/shard_map/ppermute | solution.py:18
  33.4 1.3 copy-start.4
  34.6 0.9 copy-start.5
  35.6 51.7 %copy-start.2 = (bf16[1,256,1792]{2,1,0:T(8,128)(2,1)S(1)}, bf16[1,256,1792]{2,1,0:T(8,128)(2,1)}, u32[]{:S(2)}) copy-start(bf16[1,256,1792]{2,1,0:T(8,128)(2,1)} %param.7) | copy-start | bytes 2752516
  90.3 214.8 %all-reduce.5.cloned.1.call-start = ((), (), s32[]{:S(2)}) async-start(), calls=%async_computation.3 | async-start | bytes 2097152 | tf_op jit(solution)/shard_map/psum | solution.py:128
  163.4 141.6 %copy-start = (f32[256,512]{1,0:T(8,128)S(1)}, f32[256,512]{1,0:T(8,128)}, u32[]{:S(2)}) copy-start(f32[256,512]{1,0:T(8,128)} %all-reduce.3.cloned.1.call-done.p_ref) | copy-start | bytes 1572868
  166.8 241.2 %reduce-scatter.2.cloned.1.call-start = ((), (), s32[]{:S(2)}) async-start(), calls=%async_computation.4 | async-start | bytes 3899392 | tf_op jit(solution)/shard_map/reduce_scatter | solution.py:134
  305.0 1.2 copy-start.1
  333.0 159.2 %copy-start.3 = (bf16[256,512]{1,0:T(8,128)(2,1)S(1)}, bf16[256,512]{1,0:T(8,128)(2,1)}, u32[]{:S(2)}) copy-start(bf16[256,512]{1,0:T(8,128)(2,1)} %shard_map.84) | copy-start | bytes 786436
  333.0 159.1 %all-gather.5.cloned.1.call-start = ((), (), s32[]{:S(2)}) async-start(), calls=%async_computation.5 | async-start | bytes 1949696 | tf_op jit(solution)/shard_map/all_gather | solution.py:142
Sparse Core Ops, SparseCore 0:
  10.1 77.1 all-gather.2
  90.4 72.9 all-reduce.2
  166.9 138.1 all-reduce.4
  333.1 74.7 reduce-scatter.1
  423.3 68.7 all-gather.4

commit v2 on v1

--- a/solution.py
+++ b/solution.py
@@ -7,20 +7,6 @@
 
 D = 4096
 FF = 14336
-
-
-def extended(block, sides, width):
-    for axis, dim in sides:
-        count = lax.axis_size(axis)
-        forward = [(i, i + 1) for i in range(count - 1)]
-        forward.append((count - 1, 0))
-        backward = [(target, source) for source, target in forward]
-        low = lax.ppermute(
-            lax.slice_in_dim(block, block.shape[dim] - width, None, axis=dim), axis, forward
-        )
-        high = lax.ppermute(lax.slice_in_dim(block, 0, width, axis=dim), axis, backward)
-        block = jnp.concatenate([low, block, high], axis=dim)
-    return block
 
 
 NB = 128
@@ -104,46 +90,290 @@
     )(gram, pmat)
 
 
+MESH = pl.DeviceIdType.MESH
+Z, Y, T = 16, 4, 8
+BF = jnp.bfloat16
+F32 = jnp.float32
+
+
+def ds(start, size):
+    return pl.ds(pl.multiple_of(start, size), size)
+
+
+def push(src, dst, ssem, rsem, **where):
+    copy = pltpu.make_async_remote_copy(
+        src_ref=src, dst_ref=dst, send_sem=ssem, recv_sem=rsem, device_id=where, device_id_type=MESH
+    )
+    copy.start()
+    return copy
+
+
+def enter(peers):
+    barrier = pltpu.get_barrier_semaphore()
+    for where in peers:
+        pl.semaphore_signal(barrier, inc=1, device_id=where, device_id_type=MESH)
+    pl.semaphore_wait(barrier, len(peers))
+
+
+def ring_gather(first, full, ssem, rsem):
+    me = lax.axis_index("fsdp")
+    right, left = lax.rem(me + 1, Z), lax.rem(me + Z - 1, Z)
+    sent = []
+    last = {}
+    for s in range(Z // 2):
+        for h in range(2):
+            for way in range(2):
+                if way == 1 and s == Z // 2 - 1:
+                    continue
+                owner = lax.rem(me - s + Z, Z) if way == 0 else lax.rem(me + s, Z)
+                dst = full.at[ds(owner * 32 + 16 * h, 16), :]
+                if s > 0:
+                    last[h, way].wait_recv()
+                src = first.at[16 * h:16 * h + 16, :] if s == 0 else dst
+                copy = push(src, dst, ssem.at[way, s, h], rsem.at[way, s, h], fsdp=right if way == 0 else left)
+                last[h, way] = copy
+                sent.append(copy)
+    for copy in last.values():
+        copy.wait_recv()
+    return sent
+
+
+def y_gather(view, partner_too, ssem, rsem, psend, precv):
+    tp = lax.axis_index("tp")
+    y, core = tp // 2, lax.rem(tp, 2)
+    other = tp + 1 - 2 * core
+    up, down, far = lax.rem(y + 1, Y), lax.rem(y + Y - 1, Y), lax.rem(y + 2, Y)
+    sent = []
+    cross = []
+    halves = {}
+    for h in range(2):
+        for way, goal in ((0, up), (1, down)):
+            copy = push(view(y, core, h), view(y, core, h), ssem.at[way, h], rsem.at[way, h], tp=goal * 2 + core)
+            halves[way, h] = copy
+            sent.append(copy)
+    for h in range(2):
+        cross.append(push(view(y, core, h), view(y, core, h), psend.at[0, h], precv.at[0, h], tp=other))
+    for h in (0, 1):
+        way = h
+        origin, goal = (down, up) if way == 0 else (up, down)
+        halves[way, h].wait_recv()
+        copy = push(view(origin, core, h), view(origin, core, h), ssem.at[2, h], rsem.at[2, h], tp=goal * 2 + core)
+        halves[2, h] = copy
+        sent.append(copy)
+        cross.append(push(view(origin, core, h), view(origin, core, h), psend.at[1 + way, h], precv.at[1 + way, h], tp=other))
+    for way, h in ((0, 1), (1, 0)):
+        origin = down if way == 0 else up
+        halves[way, h].wait_recv()
+        cross.append(push(view(origin, core, h), view(origin, core, h), psend.at[1 + way, h], precv.at[1 + way, h], tp=other))
+    for h in range(2):
+        halves[2, h].wait_recv()
+        cross.append(push(view(far, core, h), view(far, core, h), psend.at[3, h], precv.at[3, h], tp=other))
+    for copy in cross:
+        copy.wait_recv()
+    return sent + cross
+
+
+def front_kernel(mix_ref, tr_ref, gd_ref, mo_ref, q_ref, nt_ref, ab_ref, ac_ref, p_ref, g_ref,
+                 tlo, thi, qfull, part, rx1, half, rx2, own, gw, gp, rg,
+                 xs, xr, qs, qr, cs, cr, ys, yr, ags, agr, aps, apr, zs, zr, gs, gr, hs, hr, hps, hpr):
+    x = lax.axis_index("rep")
+    z = lax.axis_index("fsdp")
+    tp = lax.axis_index("tp")
+    y, core = tp // 2, lax.rem(tp, 2)
+    other = tp + 1 - 2 * core
+    xn = lax.axis_size("rep")
+    xu, xd = lax.rem(x + 1, xn), lax.rem(x + xn - 1, xn)
+    zu, zd = lax.rem(z + 1, Z), lax.rem(z + Z - 1, Z)
+    ypeers = [lax.rem(y + d, Y) * 2 + core for d in range(1, Y)]
+    enter([{"rep": xu}, {"rep": xd}, {"fsdp": zu}, {"fsdp": zd}, {"tp": other}] + [{"tp": t} for t in ypeers])
+    sent = []
+    up = push(tr_ref, tlo, xs.at[0], xr.at[0], rep=xu)
+    down = push(tr_ref, thi, xs.at[1], xr.at[1], rep=xd)
+    sent += [up, down]
+    qfull[ds(z * 32, 32), :] = q_ref[...]
+    sent += ring_gather(q_ref, qfull, qs, qr)
+    up.wait_recv()
+    down.wait_recv()
+    c = [jnp.full((8, 128), mix_ref[x, i].astype(F32)) for i in range(3)]
+    total = c[0] + c[1] + c[2]
+    w = [(v / total)[0:1, 0:1] for v in c]
+
+    def mixing(i, _):
+        r = ds(i * 16, 16)
+        tracked = (
+            w[0] * tr_ref[r, :].astype(F32) + w[1] * tlo[r, :].astype(F32) + w[2] * thi[r, :].astype(F32)
+        ) + gd_ref[r, :].astype(F32)
+        accum = mo_ref[r, :].astype(F32) + tracked
+        nt_ref[r, :] = tracked.astype(BF)
+        ac_ref[r, :] = accum
+        ab_ref[r, :] = accum.astype(BF)
+        return 0
+
+    lax.fori_loop(0, tr_ref.shape[0] // 16, mixing, 0)
+    for n in range(2):
+        part[:, 256 * n:256 * n + 256] = lax.dot_general(
+            ab_ref[...], qfull[256 * n:256 * n + 256, :], (((1,), (1,)), ((), ())), preferred_element_type=F32
+        )
+    swap = push(part.at[ds((1 - core) * 128, 128), :], rx1, cs, cr, tp=other)
+    sent.append(swap)
+    swap.wait_recv()
+    half[...] = part[ds(core * 128, 128), :] + rx1[...]
+    shares = []
+    for d in range(1, Y):
+        yd = lax.rem(y + d, Y)
+        shares.append(push(half.at[ds(yd * 32, 32), :], rx2.at[d - 1], ys.at[d - 1], yr.at[d - 1], tp=yd * 2 + core))
+    sent += shares
+    for copy in shares:
+        copy.wait_recv()
+    p_ref[ds(core * 128 + y * 32, 32), :] = ((half[ds(y * 32, 32), :] + rx2[0]) + rx2[1]) + rx2[2]
+
+    def pview(yy, cc, h):
+        return p_ref.at[ds(cc * 128 + yy * 32 + 16 * h, 16), :]
+
+    sent += y_gather(pview, True, ags, agr, aps, apr)
+    gw[...] = lax.dot_general(
+        p_ref[:, ds(y * 128, 128)], p_ref[...], (((0,), (0,)), ((), ())), precision=HI, preferred_element_type=F32
+    )
+    gp[...] = gw[ds(core * 64, 64), :]
+
+    def piece(ref, base, zz):
+        return ref.at[ds(base + 8 * (zz // 2), 8), ds(256 * lax.rem(zz, 2), 256)]
+
+    pieces = []
+    for d in range(1, Z):
+        zz = lax.rem(z + d, Z)
+        pieces.append(push(piece(gp, 0, zz), rg.at[d - 1], zs.at[d - 1], zr.at[d - 1], fsdp=zz))
+    sent += pieces
+    acc = gp[ds(8 * (z // 2), 8), ds(256 * lax.rem(z, 2), 256)]
+    for d in range(1, Z):
+        pieces[d - 1].wait_recv()
+        acc = acc + rg[d - 1]
+    base = y * 128 + core * 64
+    g_ref[ds(base + 8 * (z // 2), 8), ds(256 * lax.rem(z, 2), 256)] = acc
+    out = []
+    for d in range(1, Z):
+        zz = lax.rem(z + d, Z)
+        out.append(push(piece(g_ref, base, z), piece(g_ref, base, z), gs.at[d - 1], gr.at[d - 1], fsdp=zz))
+    sent += out
+    for copy in out:
+        copy.wait_recv()
+
+    def gview(yy, cc, h):
+        return g_ref.at[ds(yy * 128 + cc * 64 + 32 * h, 32), :]
+
+    sent += y_gather(gview, True, hs, hr, hps, hpr)
+    for copy in sent:
+        copy.wait_send()
+
+
+VM = pl.BlockSpec(memory_space=pltpu.VMEM)
+DMA = pltpu.SemaphoreType.DMA
+
+
+def front(mix, tracker, grad, momentum, q_t):
+    rows, cols = tracker.shape
+    rank = q_t.shape[0] * Z
+    sd = jax.ShapeDtypeStruct
+    vm = pltpu.VMEM
+    return pl.pallas_call(
+        front_kernel,
+        out_shape=(sd((rows, cols), BF), sd((rows, cols), BF), sd((rows, cols), F32), sd((rows, rank), F32), sd((rank, rank), F32)),
+        in_specs=[pl.BlockSpec(memory_space=pltpu.SMEM)] + [VM] * 4,
+        out_specs=(VM,) * 5,
+        scratch_shapes=[
+            vm((rows, cols), BF), vm((rows, cols), BF), vm((rank, cols), BF), vm((rows, rank), F32),
+            vm((128, rank), F32), vm((128, rank), F32), vm((3, 32, rank), F32), vm((32, rank), F32),
+            vm((128, rank), F32), vm((64, rank), F32), vm((15, 8, 256), F32),
+            DMA((2,)), DMA((2,)), DMA((2, 8, 2)), DMA((2, 8, 2)), DMA, DMA, DMA((3,)), DMA((3,)),
+            DMA((3, 2)), DMA((3, 2)), DMA((4, 2)), DMA((4, 2)),
+            DMA((15,)), DMA((15,)), DMA((15,)), DMA((15,)),
+            DMA((3, 2)), DMA((3, 2)), DMA((4, 2)), DMA((4, 2)),
+        ],
+        compiler_params=pltpu.CompilerParams(collective_id=0, has_side_effects=True, vmem_limit_bytes=48 << 20),
+    )(mix, tracker, grad, momentum, q_t)
+
+
+def back_kernel(lb_ref, ab_ref, ac_ref, qn_ref, nm_ref, prod, sbuf, rbuf, rb, rfull, sq, sqr,
+                rs, rr, gs, gr, ss, sr):
+    me = lax.axis_index("fsdp")
+    tp = lax.axis_index("tp")
+    right, left = lax.rem(me + 1, Z), lax.rem(me + Z - 1, Z)
+    peers = [lax.rem(tp + d, T) for d in range(1, T)]
+    enter([{"fsdp": right}, {"fsdp": left}] + [{"tp": t} for t in peers])
+    cols = ab_ref.shape[1]
+    scale = 1.0 / D ** 0.5
+    for n in range(cols // 256):
+        prod[:, 256 * n:256 * n + 256] = lax.dot_general(
+            lb_ref[...], ab_ref[:, 256 * n:256 * n + 256], (((0,), (0,)), ((), ())), preferred_element_type=F32
+        ) * scale
+    sent = []
+    last = {}
+    for s in range(Z // 2):
+        for h in range(2):
+            for way in range(2):
+                if way == 0 and s == Z // 2 - 1:
+                    continue
+                goal = lax.rem(me + 7 - s, Z) if way == 0 else lax.rem(me + Z - 8 + s, Z)
+                term = prod[ds(goal * 32 + 16 * h, 16), :]
+                if s > 0:
+                    last[h, way].wait_recv()
+                    term = term + rbuf[way, s - 1, 16 * h:16 * h + 16, :].astype(F32)
+                sbuf[way, s, 16 * h:16 * h + 16, :] = term.astype(BF)
+                copy = push(
+                    sbuf.at[way, s, 16 * h:16 * h + 16, :], rbuf.at[way, s, 16 * h:16 * h + 16, :],
+                    rs.at[way, s, h], rr.at[way, s, h], fsdp=right if way == 0 else left,
+                )
+                last[h, way] = copy
+                sent.append(copy)
+    for copy in last.values():
+        copy.wait_recv()
+    mine = prod[ds(me * 32, 32), :] + rbuf[0, 6].astype(F32) + rbuf[1, 7].astype(F32)
+    rb[...] = mine.astype(BF)
+    rfull[ds(me * 32, 32), :] = mine.astype(BF)
+    sq[...] = jnp.broadcast_to(jnp.sum(mine * mine, axis=1, keepdims=True), sq.shape)
+    small = []
+    for d in range(1, T):
+        small.append(push(sq, sqr.at[d - 1], ss.at[d - 1], sr.at[d - 1], tp=peers[d - 1]))
+    sent += small
+    sent += ring_gather(rb, rfull, gs, gr)
+    total = sq[...]
+    for d in range(1, T):
+        small[d - 1].wait_recv()
+        total = total + sqr[d - 1]
+    rms = jnp.sqrt(total / FF) + 1e-06
+    qn_ref[...] = (mine / rms[:, 0:1]).astype(BF)
+    for n in range(cols // 256):
+        part = slice(256 * n, 256 * n + 256)
+        feed = jnp.dot(lb_ref[...], rfull[:, part], preferred_element_type=F32)
+        nm_ref[:, part] = (ac_ref[:, part] - 0.5 * scale * feed).astype(BF)
+    for copy in sent:
+        copy.wait_send()
+
+
+def back(left_b, accum_b, accum):
+    rows, cols = accum.shape
+    rank = left_b.shape[1]
+    sd = jax.ShapeDtypeStruct
+    vm = pltpu.VMEM
+    return pl.pallas_call(
+        back_kernel,
+        out_shape=(sd((32, cols), BF), sd((rows, cols), BF)),
+        in_specs=[VM] * 3,
+        out_specs=(VM,) * 2,
+        scratch_shapes=[
+            vm((rank, cols), F32), vm((2, 8, 32, cols), BF), vm((2, 8, 32, cols), BF), vm((32, cols), BF),
+            vm((rank, cols), BF), vm((32, 128), F32), vm((7, 32, 128), F32),
+            DMA((2, 8, 2)), DMA((2, 8, 2)), DMA((2, 8, 2)), DMA((2, 8, 2)), DMA((7,)), DMA((7,)),
+        ],
+        compiler_params=pltpu.CompilerParams(collective_id=1, has_side_effects=True, vmem_limit_bytes=48 << 20),
+    )(left_b, accum_b, accum)
+
+
 def local(tracker, grad_delta, momentum, q_basis, mix_counts):
-    agent = lax.axis_index("rep")
-    counts = mix_counts.astype(jnp.float32)
-    select = (jnp.arange(counts.shape[0]) == agent).astype(jnp.float32)
-    mine = jnp.sum(select[:, None] * counts, axis=0)
-    weights = mine / jnp.sum(mine)
-    near = extended(tracker, (("rep", 0),), 1)
-    mixed = (
-        weights[0] * near[1].astype(jnp.float32)
-        + weights[1] * near[0].astype(jnp.float32)
-        + weights[2] * near[2].astype(jnp.float32)
-    )
-    tracked = mixed + grad_delta[0].astype(jnp.float32)
-    new_tracker = tracked.astype(jnp.bfloat16)
-    accum = momentum[0].astype(jnp.float32) + tracked
-    accum_b = accum.astype(jnp.bfloat16)
-    scale = 1.0 / jnp.sqrt(jnp.float32(D))
-    basis_full = lax.all_gather(q_basis, "fsdp", axis=2, tiled=True)[0]
-    partial_left = jnp.dot(accum_b, basis_full, preferred_element_type=jnp.float32)
-    pmat = lax.psum(partial_left, "tp")
-    gram_part = jnp.dot(pmat.T, pmat, precision=lax.Precision.HIGHEST)
-    gram = lax.psum(gram_part, "fsdp")
+    new_tracker, accum_b, accum, pmat, gram = front(mix_counts, tracker[0], grad_delta[0], momentum[0], q_basis[0].T)
     left_b = left_solve(gram, pmat)
-    block = left_b
-    product = lax.dot_general(
-        block, accum_b, (((0,), (0,)), ((), ())), preferred_element_type=jnp.float32
-    )
-    right_t = lax.psum_scatter(product * scale, "fsdp", scatter_dimension=0, tiled=True)
-    squares = lax.psum(jnp.sum(right_t * right_t, axis=1), "tp")
-    rms = jnp.sqrt(squares / FF) + 1e-06
-    q_new = (right_t / rms[:, None]).T.astype(jnp.bfloat16)
-    right_b = right_t.astype(jnp.bfloat16)
-    block = left_b
-    feed = jnp.dot(
-        block,
-        lax.all_gather(right_b, "fsdp", axis=0, tiled=True),
-        preferred_element_type=jnp.float32,
-    )
-    new_momentum = (accum - 0.5 * scale * feed).astype(jnp.bfloat16)
-    return (new_tracker[None], new_momentum[None], left_b[None], q_new[None])
+    q_t, new_momentum = back(left_b, accum_b, accum)
+    return (new_tracker[None], new_momentum[None], left_b[None], q_t.T[None])
 
 
 def solution(mesh):

time: 502 us -> 195 us (0.39)
  waiting for transfers between devices: 416 us -> 0 us
  Pallas kernels: 23.3 us -> 182 us
  between operations: 13.8 us -> 0.68 us
  matrix products: 12.8 us -> 0 us
  blocking collectives: 12.4 us -> 0 us
  other arithmetic: 10.4 us -> 0 us
  starting transfers between devices: 9.89 us -> 0 us
  local copies, waits for them, and re-layouts: 2.81 us -> 9.91 us
    psum x2 -> x0, waiting for transfers between devices: 211 us -> none  [the longest x1 138 us: local(): gram = lax.psum(gram_part, 'fsdp')]
    pallas_call x0 -> x2, Pallas kernels: none -> 158 us  [the longest x1 90 us: front(): pl.pallas_call(front_kernel, out_shape=(sd((rows, cols), BF), sd((rows, c...]
    all_gather x2 -> x0, waiting for transfers between devices: 115 us -> none  [the longest x1 68.9 us: local(): lax.all_gather(right_b, 'fsdp', axis=0, tiled=True)]
    reduce_scatter x1 -> x0, waiting for transfers between devices: 74.8 us -> none  [local(): lax.psum_scatter(product * scale, 'fsdp', scatter_dimension=0, tiled=True)]
    ppermute x2 -> x0, waiting for transfers between devices: 14.3 us -> none  [the longest x1 13 us: extended(): lax.ppermute(lax.slice_in_dim(block, 0, width, axis=dim), axis, backward)]
    dot_general x4 -> x0, matrix products: 12.8 us -> none  [the longest x1 3.43 us: local(): lax.dot_general(block, accum_b, (((0,), (0,)), ((), ())), preferred_eleme...]
    psum x1 -> x0, blocking collectives: 12.4 us -> none  [local(): squares = lax.psum(jnp.sum(right_t * right_t, axis=1), 'tp')]
    ppermute x2 -> x0, starting transfers between devices: 9.68 us -> none  [the longest x1 6.95 us: extended(): lax.ppermute(lax.slice_in_dim(block, block.shape[dim] - width, None, axis...]
  transfers between devices with their start and end apart: 7 -> 0, of which waited for: 7 -> 0; matrix products, arithmetic and copies ran while one was open for 2% -> 0% of each run, Pallas kernels for 0% -> 0%
where the time goes in v2:
time: 195 us; the launch traced here: 192 us
  Pallas kernels  182 us (93%)
  local copies, waits for them, and re-layouts  9.91 us (5%)
    pallas_call x1, Pallas kernels, front(): pl.pallas_call(front_kernel, out_shape=(sd((rows, cols), BF), sd((rows, c...  90 us
    pallas_call x1, Pallas kernels, back(): pl.pallas_call(back_kernel, out_shape=(sd((32, cols), BF), sd((rows, cols...  68.4 us
    pallas_call x1, Pallas kernels, left_solve(): pl.pallas_call(solve_kernel, out_shape=jax.ShapeDtypeStruct((m, n), jnp.b...  23.3 us
    unnamed x19, local copies, waits for them, and re-layouts  9.91 us

profile of v2, /device:TPU:6, one launch (start us, length us, event | category | flops | bytes accessed | tf_op | source)
XLA Modules:
  0.0 192.3 jit_solution(11966976868932238334)
XLA Ops:
  0.6 0.0 copy-start.3
  0.6 1.2 copy-done.3
  1.8 0.0 copy-start.4
  1.8 1.2 copy-done.4
  3.0 0.0 copy-start.5
  3.0 1.2 copy-done.5
  4.2 0.0 copy-start.6
  4.2 0.9 copy-done.6
  5.1 0.0 copy-start.7
  5.1 0.7 copy-done.7
  5.8 90.0 %shard_map.84 = (bf16[256,1792]{1,0:T(8,128)(2,1)S(1)}, bf16[256,1792]{1,0:T(8,128)(2,1)S(1)}, f32[256,1792]{1,0:T(8,128)}, f32[256,512]{1,0:T(8,128)S(1)}, f32[512,512]{1,0:T(8,128)}) custom-call(s32[4,3]{1,0:T(4,128)S(1)} %copy-done.7, bf16[256,1792]{1,0:T(8,128)(2,1)S(1)} %bitcast.15, bf16[256,1792]{1,0:T(8,128)(2,1)S(1)} %bitcast.16, ...), custom_call_target="tpu_custom_call" | custom-call | tf_op jit(solution)/shard_map/pallas_call | solution.py:278
  95.7 0.0 copy-start
  95.7 0.0 copy-start.2
  95.7 1.3 copy-done.2
  97.1 23.3 %shard_map.85.lb_ref = bf16[256,512]{1,0:T(8,128)(2,1)} custom-call(f32[512,512]{1,0:T(8,128)S(1)} %copy-done.2, f32[256,512]{1,0:T(8,128)S(1)} %get-tuple-element.13.p_ref), custom_call_target="tpu_custom_call" | custom-call | tf_op jit(solution)/shard_map/pallas_call | solution.py:83
  120.4 0.0 copy-done
  120.4 0.0 copy-start.1
  120.4 0.9 copy-done.1
  121.3 68.4 %shard_map.86 = (bf16[32,1792]{1,0:T(8,128)(2,1)S(1)}, bf16[256,1792]{1,0:T(8,128)(2,1)S(1)}) custom-call(bf16[256,512]{1,0:T(8,128)(2,1)S(1)} %copy-done.1, bf16[256,1792]{1,0:T(8,128)(2,1)S(1)} %get-tuple-element.14.ab_ref, f32[256,1792]{1,0:T(8,128)S(1)} %copy-done), custom_call_target="tpu_custom_call" | custom-call | tf_op jit(solution)/shard_map/pallas_call | solution.py:358
  189.8 0.9 copy.12
  190.7 0.9 copy.13
  191.6 0.6 copy.14
Async XLA Ops:
  0.6 1.2 copy-start.3
  1.8 1.2 copy-start.4
  3.0 1.2 copy-start.5
  4.2 0.9 copy-start.6
  5.1 0.7 copy-start.7
  95.7 24.7 %copy-start = (f32[256,1792]{1,0:T(8,128)S(1)}, f32[256,1792]{1,0:T(8,128)}, u32[]{:S(2)}) copy-start(f32[256,1792]{1,0:T(8,128)} %get-tuple-element.15.ac_ref) | copy-start | bytes 5505028
  95.7 1.4 copy-start.2
  120.4 1.0 copy-start.1

commit v3 on v2

--- a/solution.py
+++ b/solution.py
@@ -86,7 +86,7 @@
         in_specs=[pl.BlockSpec(memory_space=pltpu.VMEM)] * 2,
         out_specs=pl.BlockSpec(memory_space=pltpu.VMEM),
         scratch_shapes=[pltpu.VMEM((n + m, n), jnp.float32), pltpu.VMEM((NB, NB), jnp.float32)],
-        compiler_params=pltpu.CompilerParams(vmem_limit_bytes=40 << 20),
+        compiler_params=pltpu.CompilerParams(vmem_limit_bytes=67043328),
     )(gram, pmat)
 
 
@@ -115,24 +115,28 @@
     pl.semaphore_wait(barrier, len(peers))
 
 
-def ring_gather(first, full, ssem, rsem):
+def ring_gather(first, full, ssem, rsem, between=None):
     me = lax.axis_index("fsdp")
     right, left = lax.rem(me + 1, Z), lax.rem(me + Z - 1, Z)
+    wide = first.shape[1] // 2
     sent = []
     last = {}
     for s in range(Z // 2):
-        for h in range(2):
+        for q in range(4):
+            h, lanes = q // 2, slice((q % 2) * wide, (q % 2) * wide + wide)
             for way in range(2):
-                if way == 1 and s == Z // 2 - 1:
+                if s == Z // 2 - 1 and way != h:
                     continue
                 owner = lax.rem(me - s + Z, Z) if way == 0 else lax.rem(me + s, Z)
-                dst = full.at[ds(owner * 32 + 16 * h, 16), :]
+                dst = full.at[ds(owner * 32 + 16 * h, 16), lanes]
                 if s > 0:
-                    last[h, way].wait_recv()
-                src = first.at[16 * h:16 * h + 16, :] if s == 0 else dst
-                copy = push(src, dst, ssem.at[way, s, h], rsem.at[way, s, h], fsdp=right if way == 0 else left)
-                last[h, way] = copy
+                    last[q, way].wait_recv()
+                src = first.at[16 * h:16 * h + 16, lanes] if s == 0 else dst
+                copy = push(src, dst, ssem.at[way, s, q], rsem.at[way, s, q], fsdp=right if way == 0 else left)
+                last[q, way] = copy
                 sent.append(copy)
+        if between is not None:
+            between(s)
     for copy in last.values():
         copy.wait_recv()
     return sent
@@ -173,8 +177,8 @@
     return sent + cross
 
 
-def front_kernel(mix_ref, tr_ref, gd_ref, mo_ref, q_ref, nt_ref, ab_ref, ac_ref, p_ref, g_ref,
-                 tlo, thi, qfull, part, rx1, half, rx2, own, gw, gp, rg,
+def front_kernel(mix_ref, tr_hbm, gd_hbm, mo_hbm, q_ref, nt_ref, ab_hbm, ac_hbm, p_ref, g_ref,
+                 tr_ref, gd_ref, mo_ref, ab_ref, ac_ref, lsem, tlo, thi, qfull, part, rx1, half, rx2, own, gw, gp, rg,
                  xs, xr, qs, qr, cs, cr, ys, yr, ags, agr, aps, apr, zs, zr, gs, gr, hs, hr, hps, hpr):
     x = lax.axis_index("rep")
     z = lax.axis_index("fsdp")
@@ -185,15 +189,21 @@
     xu, xd = lax.rem(x + 1, xn), lax.rem(x + xn - 1, xn)
     zu, zd = lax.rem(z + 1, Z), lax.rem(z + Z - 1, Z)
     ypeers = [lax.rem(y + d, Y) * 2 + core for d in range(1, Y)]
+    loads = [
+        pltpu.make_async_copy(src, dst, lsem.at[i])
+        for i, (src, dst) in enumerate(((tr_hbm, tr_ref), (gd_hbm, gd_ref), (mo_hbm, mo_ref)))
+    ]
+    for copy in loads:
+        copy.start()
     enter([{"rep": xu}, {"rep": xd}, {"fsdp": zu}, {"fsdp": zd}, {"tp": other}] + [{"tp": t} for t in ypeers])
     sent = []
-    up = push(tr_ref, tlo, xs.at[0], xr.at[0], rep=xu)
-    down = push(tr_ref, thi, xs.at[1], xr.at[1], rep=xd)
-    sent += [up, down]
-    qfull[ds(z * 32, 32), :] = q_ref[...]
-    sent += ring_gather(q_ref, qfull, qs, qr)
-    up.wait_recv()
-    down.wait_recv()
+    arrivals = []
+    for k in range(4):
+        band = slice(64 * k, 64 * k + 64)
+        up = push(tr_hbm.at[band], tlo.at[band], xs.at[0, k], xr.at[0, k], rep=xu)
+        down = push(tr_hbm.at[band], thi.at[band], xs.at[1, k], xr.at[1, k], rep=xd)
+        arrivals.append((up, down))
+        sent += [up, down]
     c = [jnp.full((8, 128), mix_ref[x, i].astype(F32)) for i in range(3)]
     total = c[0] + c[1] + c[2]
     w = [(v / total)[0:1, 0:1] for v in c]
@@ -209,17 +219,41 @@
         ab_ref[r, :] = accum.astype(BF)
         return 0
 
-    lax.fori_loop(0, tr_ref.shape[0] // 16, mixing, 0)
-    for n in range(2):
-        part[:, 256 * n:256 * n + 256] = lax.dot_general(
-            ab_ref[...], qfull[256 * n:256 * n + 256, :], (((1,), (1,)), ((), ())), preferred_element_type=F32
-        )
+    def mix_band(k):
+        if k == 0:
+            for copy in loads:
+                copy.wait()
+        for copy in arrivals[k]:
+            copy.wait_recv()
+        lax.fori_loop(4 * k, 4 * k + 4, mixing, 0)
+
+    def between(s):
+        if s in (3, 5, 7):
+            mix_band((s - 3) // 2)
+
+    sent_q = ring_gather(q_ref, qfull, qs, qr, between)
+    sent += sent_q
+    qfull[ds(z * 32, 32), :] = q_ref[...]
+    mix_band(3)
+    outs = [pltpu.make_async_copy(ab_ref, ab_hbm, lsem.at[0]), pltpu.make_async_copy(ac_ref, ac_hbm, lsem.at[1])]
+    for copy in outs:
+        copy.start()
+
+    def product(side):
+        band = ds(side * 128, 128)
+        for n in range(2):
+            part[band, 256 * n:256 * n + 256] = lax.dot_general(
+                ab_ref[band, :], qfull[256 * n:256 * n + 256, :], (((1,), (1,)), ((), ())), preferred_element_type=F32
+            )
+
+    product(1 - core)
     swap = push(part.at[ds((1 - core) * 128, 128), :], rx1, cs, cr, tp=other)
     sent.append(swap)
+    product(core)
     swap.wait_recv()
     half[...] = part[ds(core * 128, 128), :] + rx1[...]
     shares = []
-    for d in range(1, Y):
+    for d in (2, 1, 3):
         yd = lax.rem(y + d, Y)
         shares.append(push(half.at[ds(yd * 32, 32), :], rx2.at[d - 1], ys.at[d - 1], yr.at[d - 1], tp=yd * 2 + core))
     sent += shares
@@ -262,11 +296,14 @@
         return g_ref.at[ds(yy * 128 + cc * 64 + 32 * h, 32), :]
 
     sent += y_gather(gview, True, hs, hr, hps, hpr)
+    for copy in outs:
+        copy.wait()
     for copy in sent:
         copy.wait_send()
 
 
 VM = pl.BlockSpec(memory_space=pltpu.VMEM)
+HB = pl.BlockSpec(memory_space=pltpu.HBM)
 DMA = pltpu.SemaphoreType.DMA
 
 
@@ -278,56 +315,71 @@
     return pl.pallas_call(
         front_kernel,
         out_shape=(sd((rows, cols), BF), sd((rows, cols), BF), sd((rows, cols), F32), sd((rows, rank), F32), sd((rank, rank), F32)),
-        in_specs=[pl.BlockSpec(memory_space=pltpu.SMEM)] + [VM] * 4,
-        out_specs=(VM,) * 5,
+        in_specs=[pl.BlockSpec(memory_space=pltpu.SMEM)] + [HB] * 3 + [VM],
+        out_specs=(VM, HB, HB, VM, VM),
         scratch_shapes=[
+            vm((rows, cols), BF), vm((rows, cols), BF), vm((rows, cols), BF), vm((rows, cols), BF), vm((rows, cols), F32), DMA((3,)),
             vm((rows, cols), BF), vm((rows, cols), BF), vm((rank, cols), BF), vm((rows, rank), F32),
             vm((128, rank), F32), vm((128, rank), F32), vm((3, 32, rank), F32), vm((32, rank), F32),
             vm((128, rank), F32), vm((64, rank), F32), vm((15, 8, 256), F32),
-            DMA((2,)), DMA((2,)), DMA((2, 8, 2)), DMA((2, 8, 2)), DMA, DMA, DMA((3,)), DMA((3,)),
+            DMA((2, 4)), DMA((2, 4)), DMA((2, 8, 4)), DMA((2, 8, 4)), DMA, DMA, DMA((3,)), DMA((3,)),
             DMA((3, 2)), DMA((3, 2)), DMA((4, 2)), DMA((4, 2)),
             DMA((15,)), DMA((15,)), DMA((15,)), DMA((15,)),
             DMA((3, 2)), DMA((3, 2)), DMA((4, 2)), DMA((4, 2)),
         ],
-        compiler_params=pltpu.CompilerParams(collective_id=0, has_side_effects=True, vmem_limit_bytes=48 << 20),
+        compiler_params=pltpu.CompilerParams(collective_id=0, has_side_effects=True, vmem_limit_bytes=67043328),
     )(mix, tracker, grad, momentum, q_t)
 
 
-def back_kernel(lb_ref, ab_ref, ac_ref, qn_ref, nm_ref, prod, sbuf, rbuf, rb, rfull, sq, sqr,
+def back_kernel(lb_ref, ab_hbm, ac_hbm, qn_ref, nm_ref, ab_ref, ac_ref, lsem, lt, prod, sbuf, rbuf, rb, rfull, sq, sqr,
                 rs, rr, gs, gr, ss, sr):
     me = lax.axis_index("fsdp")
     tp = lax.axis_index("tp")
     right, left = lax.rem(me + 1, Z), lax.rem(me + Z - 1, Z)
     peers = [lax.rem(tp + d, T) for d in range(1, T)]
+    load_b = pltpu.make_async_copy(ab_hbm, ab_ref, lsem.at[0])
+    load_a = pltpu.make_async_copy(ac_hbm, ac_ref, lsem.at[1])
+    load_b.start()
+    load_a.start()
+    lt[...] = lb_ref[...].T
     enter([{"fsdp": right}, {"fsdp": left}] + [{"tp": t} for t in peers])
     cols = ab_ref.shape[1]
+    wide = cols // 2
     scale = 1.0 / D ** 0.5
-    for n in range(cols // 256):
-        prod[:, 256 * n:256 * n + 256] = lax.dot_general(
-            lb_ref[...], ab_ref[:, 256 * n:256 * n + 256], (((0,), (0,)), ((), ())), preferred_element_type=F32
-        ) * scale
+    load_b.wait()
     sent = []
     last = {}
     for s in range(Z // 2):
-        for h in range(2):
+        if s == 0:
+            far = jnp.dot(lt[ds(lax.rem(me + 8, Z) * 32, 32), :], ab_ref[...], preferred_element_type=F32) * scale
+        for q in range(4):
+            h, lanes = q // 2, slice((q % 2) * wide, (q % 2) * wide + wide)
             for way in range(2):
-                if way == 0 and s == Z // 2 - 1:
+                if s == 0 and way != h:
                     continue
-                goal = lax.rem(me + 7 - s, Z) if way == 0 else lax.rem(me + Z - 8 + s, Z)
-                term = prod[ds(goal * 32 + 16 * h, 16), :]
-                if s > 0:
-                    last[h, way].wait_recv()
-                    term = term + rbuf[way, s - 1, 16 * h:16 * h + 16, :].astype(F32)
-                sbuf[way, s, 16 * h:16 * h + 16, :] = term.astype(BF)
+                rows = slice(16 * h, 16 * h + 16)
+                if s == 0:
+                    term = far[rows, lanes]
+                else:
+                    goal = lax.rem(me + 8 - s, Z) if way == 0 else lax.rem(me + Z - 8 + s, Z)
+                    term = prod[ds(goal * 32 + 16 * h, 16), lanes]
+                    if (q, way) in last:
+                        last[q, way].wait_recv()
+                        term = term + rbuf[way, s - 1, rows, lanes].astype(F32)
+                sbuf[way, s, rows, lanes] = term.astype(BF)
                 copy = push(
-                    sbuf.at[way, s, 16 * h:16 * h + 16, :], rbuf.at[way, s, 16 * h:16 * h + 16, :],
-                    rs.at[way, s, h], rr.at[way, s, h], fsdp=right if way == 0 else left,
+                    sbuf.at[way, s, rows, lanes], rbuf.at[way, s, rows, lanes],
+                    rs.at[way, s, q], rr.at[way, s, q], fsdp=right if way == 0 else left,
                 )
-                last[h, way] = copy
+                last[q, way] = copy
                 sent.append(copy)
+        if s == 0:
+            for n in range(cols // 256):
+                part = slice(256 * n, 256 * n + 256)
+                prod[:, part] = jnp.dot(lt[...], ab_ref[:, part], preferred_element_type=F32) * scale
     for copy in last.values():
         copy.wait_recv()
-    mine = prod[ds(me * 32, 32), :] + rbuf[0, 6].astype(F32) + rbuf[1, 7].astype(F32)
+    mine = prod[ds(me * 32, 32), :] + rbuf[0, 7].astype(F32) + rbuf[1, 7].astype(F32)
     rb[...] = mine.astype(BF)
     rfull[ds(me * 32, 32), :] = mine.astype(BF)
     sq[...] = jnp.broadcast_to(jnp.sum(mine * mine, axis=1, keepdims=True), sq.shape)
@@ -342,6 +394,7 @@
         total = total + sqr[d - 1]
     rms = jnp.sqrt(total / FF) + 1e-06
     qn_ref[...] = (mine / rms[:, 0:1]).astype(BF)
+    load_a.wait()
     for n in range(cols // 256):
         part = slice(256 * n, 256 * n + 256)
         feed = jnp.dot(lb_ref[...], rfull[:, part], preferred_element_type=F32)
@@ -358,14 +411,15 @@
     return pl.pallas_call(
         back_kernel,
         out_shape=(sd((32, cols), BF), sd((rows, cols), BF)),
-        in_specs=[VM] * 3,
+        in_specs=[VM, HB, HB],
         out_specs=(VM,) * 2,
         scratch_shapes=[
+            vm((rows, cols), BF), vm((rows, cols), F32), DMA((2,)), vm((rank, rows), BF),
             vm((rank, cols), F32), vm((2, 8, 32, cols), BF), vm((2, 8, 32, cols), BF), vm((32, cols), BF),
             vm((rank, cols), BF), vm((32, 128), F32), vm((7, 32, 128), F32),
-            DMA((2, 8, 2)), DMA((2, 8, 2)), DMA((2, 8, 2)), DMA((2, 8, 2)), DMA((7,)), DMA((7,)),
+            DMA((2, 8, 4)), DMA((2, 8, 4)), DMA((2, 8, 4)), DMA((2, 8, 4)), DMA((7,)), DMA((7,)),
         ],
-        compiler_params=pltpu.CompilerParams(collective_id=1, has_side_effects=True, vmem_limit_bytes=48 << 20),
+        compiler_params=pltpu.CompilerParams(collective_id=1, has_side_effects=True, vmem_limit_bytes=67043328),
     )(left_b, accum_b, accum)
 
 

time: 195 us -> 186 us (0.954); the launches traced: 192 us -> 186 us
  local copies, waits for them, and re-layouts: 9.91 us -> 3.82 us
    unnamed x19 -> x7, local copies, waits for them, and re-layouts: 9.91 us -> 3.82 us
where the time goes in v3:
time: 186 us
  Pallas kernels  181 us (97%)
  local copies, waits for them, and re-layouts  3.82 us (2%)
    pallas_call x1, Pallas kernels, front(): pl.pallas_call(front_kernel, out_shape=(sd((rows, cols), BF), sd((rows, c...  88.8 us
    pallas_call x1, Pallas kernels, back(): pl.pallas_call(back_kernel, out_shape=(sd((32, cols), BF), sd((rows, cols...  67.7 us
    pallas_call x1, Pallas kernels, left_solve(): pl.pallas_call(solve_kernel, out_shape=jax.ShapeDtypeStruct((m, n), jnp.b...  24.7 us
    unnamed x7, local copies, waits for them, and re-layouts  3.82 us

profile of v3, /device:TPU:6, one launch (start us, length us, event | category | flops | bytes accessed | tf_op | source)
XLA Modules:
  0.0 185.6 jit_solution(11938581240676413977)
XLA Ops:
  0.6 88.8 %shard_map.84 = (bf16[256,1792]{1,0:T(8,128)(2,1)}, bf16[256,1792]{1,0:T(8,128)(2,1)}, f32[256,1792]{1,0:T(8,128)}, f32[256,512]{1,0:T(8,128)}, f32[512,512]{1,0:T(8,128)}) custom-call(s32[4,3]{1,0:T(4,128)} %mix_ref.1, bf16[256,1792]{1,0:T(8,128)(2,1)} %bitcast.15, bf16[256,1792]{1,0:T(8,128)(2,1)} %bitcast.16, bf16[256,1792]{1,0:T(8,128)(2,1)} %bitcast.17, ...), custom_call_target="tpu_custom_call" | custom-call | tf_op jit(solution)/shard_map/pallas_call | solution.py:315
  89.4 24.7 %shard_map.85.lb_ref = bf16[256,512]{1,0:T(8,128)(2,1)} custom-call(f32[512,512]{1,0:T(8,128)} %get-tuple-element.12.g_ref, f32[256,512]{1,0:T(8,128)} %get-tuple-element.13.p_ref), custom_call_target="tpu_custom_call" | custom-call | tf_op jit(solution)/shard_map/pallas_call | solution.py:83
  114.1 67.7 %shard_map.86 = (bf16[32,1792]{1,0:T(8,128)(2,1)}, bf16[256,1792]{1,0:T(8,128)(2,1)}) custom-call(bf16[256,512]{1,0:T(8,128)(2,1)} %shard_map.85.lb_ref, bf16[256,1792]{1,0:T(8,128)(2,1)} %get-tuple-element.14.ab_hbm, f32[256,1792]{1,0:T(8,128)} %get-tuple-element.15.ac_hbm), custom_call_target="tpu_custom_call" | custom-call | tf_op jit(solution)/shard_map/pallas_call | solution.py:411
  181.8 0.0 copy-start
  181.8 0.0 copy-start.1
  181.8 2.2 %copy.12 = bf16[1,256,1792]{2,1,0:T(8,128)(2,1)} copy(bf16[1,256,1792]{2,1,0:T(8,128)(2,1)} %bitcast.13) | data formatting | bytes 1835008
  184.0 0.0 copy-done
  184.1 0.9 copy.13
  185.0 0.0 copy-done.1
  185.0 0.6 copy.14
Async XLA Ops:
  181.8 2.3 %copy-start = (bf16[256,1792]{1,0:T(8,128)(2,1)S(1)}, bf16[256,1792]{1,0:T(8,128)(2,1)}, u32[]{:S(2)}) copy-start(bf16[256,1792]{1,0:T(8,128)(2,1)} %get-tuple-element.16) | copy-start | bytes 2752516
  181.8 3.2 %copy-start.1 = (bf16[32,1792]{1,0:T(8,128)(2,1)S(1)}, bf16[32,1792]{1,0:T(8,128)(2,1)}, u32[]{:S(2)}) copy-start(bf16[32,1792]{1,0:T(8,128)(2,1)} %get-tuple-element.17) | copy-start | bytes 344068

commit v4 on v3

--- a/solution.py
+++ b/solution.py
@@ -54,8 +54,22 @@
 def nt(a, b):
     return lax.dot_general(a, b, (((1,), (1,)), ((), ())), precision=HI, preferred_element_type=jnp.float32)
 
-def solve_kernel(g_ref, p_ref, o_ref, t_ref, w_ref):
+def split(x):
+    high = x.astype(jnp.bfloat16)
+    return high, (x - high.astype(jnp.float32)).astype(jnp.bfloat16)
+
+
+def nt_split(a, b):
+    (ah, al), (bh, bl) = split(a), split(b)
+    one = lambda x, y: lax.dot_general(x, y, (((1,), (1,)), ((), ())), preferred_element_type=jnp.float32)
+    return one(ah, bh) + (one(ah, bl) + one(al, bh))
+
+
+def solve_kernel(g_ref, p_ref, nt_hbm, o_ref, nt_out, t_ref, w_ref, stage, sem):
     n = g_ref.shape[0]
+    fetch = pltpu.make_async_copy(nt_hbm, stage, sem.at[0])
+    flush = pltpu.make_async_copy(stage, nt_out, sem.at[1])
+    fetch.start()
     m = p_ref.shape[0]
     K = n // NB
     t_ref[0:n, :] = g_ref[...]
@@ -70,24 +84,31 @@
         for kk in range(K):
             @pl.when(k == kk)
             def _():
+                if kk == 1:
+                    fetch.wait()
+                    flush.start()
                 lo, hi = kk * NB, (kk + 1) * NB
-                x = nt(t_ref[hi:, lo:hi], w_ref[...])
-                o_ref[:, lo:hi] = (x[n - hi:] * D ** 0.5).astype(jnp.bfloat16)
+                y = nt_split(t_ref[n:, lo:hi], w_ref[...])
+                o_ref[:, lo:hi] = (y * D ** 0.5).astype(jnp.bfloat16)
                 if kk + 1 < K:
-                    t_ref[hi:, hi:] = t_ref[hi:, hi:] - nt(x, x[:n - hi])
+                    x = nt(t_ref[hi:n, lo:hi], w_ref[...])
+                    t_ref[hi:n, hi:] = t_ref[hi:n, hi:] - nt(x, x)
+                    t_ref[n:, hi:] = t_ref[n:, hi:] - nt_split(y, x)
         return 0
     lax.fori_loop(0, K, step, 0)
-
-def left_solve(gram, pmat):
+    flush.wait()
+
+def left_solve(gram, pmat, tracker):
     n, m = gram.shape[0], pmat.shape[0]
     return pl.pallas_call(
         solve_kernel,
-        out_shape=jax.ShapeDtypeStruct((m, n), jnp.bfloat16),
-        in_specs=[pl.BlockSpec(memory_space=pltpu.VMEM)] * 2,
-        out_specs=pl.BlockSpec(memory_space=pltpu.VMEM),
-        scratch_shapes=[pltpu.VMEM((n + m, n), jnp.float32), pltpu.VMEM((NB, NB), jnp.float32)],
+        out_shape=(jax.ShapeDtypeStruct((m, n), jnp.bfloat16), jax.ShapeDtypeStruct(tracker.shape, jnp.bfloat16)),
+        in_specs=[pl.BlockSpec(memory_space=pltpu.VMEM)] * 2 + [pl.BlockSpec(memory_space=pltpu.HBM)],
+        out_specs=(pl.BlockSpec(memory_space=pltpu.VMEM), pl.BlockSpec(memory_space=pltpu.HBM)),
+        scratch_shapes=[pltpu.VMEM((n + m, n), jnp.float32), pltpu.VMEM((NB, NB), jnp.float32),
+                        pltpu.VMEM(tracker.shape, jnp.bfloat16), pltpu.SemaphoreType.DMA((2,))],
         compiler_params=pltpu.CompilerParams(vmem_limit_bytes=67043328),
-    )(gram, pmat)
+    )(gram, pmat, tracker)
 
 
 MESH = pl.DeviceIdType.MESH
@@ -425,7 +446,7 @@
 
 def local(tracker, grad_delta, momentum, q_basis, mix_counts):
     new_tracker, accum_b, accum, pmat, gram = front(mix_counts, tracker[0], grad_delta[0], momentum[0], q_basis[0].T)
-    left_b = left_solve(gram, pmat)
+    left_b, new_tracker = left_solve(gram, pmat, new_tracker)
     q_t, new_momentum = back(left_b, accum_b, accum)
     return (new_tracker[None], new_momentum[None], left_b[None], q_t.T[None])
 

time: 186 us -> 184 us (0.989)
    unnamed x7 -> x4, local copies, waits for them, and re-layouts: 3.82 us -> 2.85 us
where the time goes in v4:
time: 184 us; the launch traced here: 183 us
  Pallas kernels  180 us (98%)
  local copies, waits for them, and re-layouts  2.85 us (2%)
    pallas_call x1, Pallas kernels, front(): pl.pallas_call(front_kernel, out_shape=(sd((rows, cols), BF), sd((rows, c...  88.7 us
    pallas_call x1, Pallas kernels, back(): pl.pallas_call(back_kernel, out_shape=(sd((32, cols), BF), sd((rows, cols...  67.6 us
    pallas_call x1, Pallas kernels, left_solve(): pl.pallas_call(solve_kernel, out_shape=(jax.ShapeDtypeStruct((m, n), jnp....  23.6 us

profile of v4, /device:TPU:6, one launch (start us, length us, event | category | flops | bytes accessed | tf_op | source)
XLA Modules:
  0.0 183.4 jit_solution(4579597424334985406)
XLA Ops:
  0.6 88.7 %shard_map.84 = (bf16[256,1792]{1,0:T(8,128)(2,1)}, bf16[256,1792]{1,0:T(8,128)(2,1)}, f32[256,1792]{1,0:T(8,128)}, f32[256,512]{1,0:T(8,128)}, f32[512,512]{1,0:T(8,128)}) custom-call(s32[4,3]{1,0:T(4,128)} %mix_ref.1, bf16[256,1792]{1,0:T(8,128)(2,1)} %bitcast.13, bf16[256,1792]{1,0:T(8,128)(2,1)} %bitcast.14, bf16[256,1792]{1,0:T(8,128)(2,1)} %bitcast.15, ...), custom_call_target="tpu_custom_call" | custom-call | tf_op jit(solution)/shard_map/pallas_call | solution.py:336
  89.3 23.6 %shard_map.85 = (bf16[256,512]{1,0:T(8,128)(2,1)}, bf16[256,1792]{1,0:T(8,128)(2,1)}) custom-call(f32[512,512]{1,0:T(8,128)} %get-tuple-element.13.g_ref, f32[256,512]{1,0:T(8,128)} %get-tuple-element.14.p_ref, bf16[256,1792]{1,0:T(8,128)(2,1)} %get-tuple-element.15.nt_hbm), custom_call_target="tpu_custom_call" | custom-call | tf_op jit(solution)/shard_map/pallas_call | solution.py:103
  112.9 67.6 %shard_map.86 = (bf16[32,1792]{1,0:T(8,128)(2,1)}, bf16[256,1792]{1,0:T(8,128)(2,1)}) custom-call(bf16[256,512]{1,0:T(8,128)(2,1)} %get-tuple-element.17.lb_ref, bf16[256,1792]{1,0:T(8,128)(2,1)} %get-tuple-element.18.ab_hbm, f32[256,1792]{1,0:T(8,128)} %get-tuple-element.19.ac_hbm), custom_call_target="tpu_custom_call" | custom-call | tf_op jit(solution)/shard_map/pallas_call | solution.py:432
  180.5 0.0 copy-start
  180.5 2.2 %copy.11 = bf16[1,256,1792]{2,1,0:T(8,128)(2,1)} copy(bf16[1,256,1792]{2,1,0:T(8,128)(2,1)} %bitcast.12) | data formatting | bytes 1835008
  182.7 0.0 copy-done
  182.7 0.6 copy.12
Async XLA Ops:
  180.5 2.2 %copy-start = (bf16[32,1792]{1,0:T(8,128)(2,1)S(1)}, bf16[32,1792]{1,0:T(8,128)(2,1)}, u32[]{:S(2)}) copy-start(bf16[32,1792]{1,0:T(8,128)(2,1)} %get-tuple-element.21) | copy-start | bytes 344068
